TPU v7x, 256 devices: a whole 4x4x8 slice. The times are simulated.
256 devices in a mesh: gen: 8 (over z_lo, core), user: 16 (over x, y), cand: 2 (over z_hi).
Axes of the slice: x: 4, y: 4, z: 8 (z_hi: 2, z_lo: 4; z = z_hi * 4 + z_lo), core: 2. Of those that a mesh axis runs over, the one named last changes fastest.
Arguments:
- states: bfloat16 [16384, 4096], P(('user', 'cand')), may hold values from -6 to 6
- norm_gain: float32 [4096], replicated, may hold values from 0.1 to 1.9
- gate_weight: bfloat16 [4096, 7168], P('user', 'gen'), may hold values from -0.09375 to 0.09375
- up_weight: bfloat16 [4096, 7168], P('user', 'gen'), may hold values from -0.09375 to 0.09375
- down_weight: bfloat16 [7168, 4096], P('gen', 'user'), may hold values from -0.0625 to 0.0625
- proj_weight: bfloat16 [4096, 1024], P('gen'), may hold values from -0.09375 to 0.09375
- private_rows: bfloat16 [32768, 1024], P(('gen', 'user')), may hold values from -6 to 6
- enc_weight: bfloat16 [1024, 1024], replicated, may hold values from -0.1875 to 0.1875
- user_ids: int32 [32768], P(('gen', 'user')), may hold values from 0 to 31
Outputs:
- votes: float32 [16, 2, 128], P(None, 'cand')
Inputs may be any that keep to these rules, and one draw needn't show every extreme that they name: `user_ids`: a user is a pair of a block of 256 rows and a slot; no user has rows in two blocks.
All inputs are finite; a program needn't handle non-finite values.
Results may differ from a plain program's by a relative error of at most 0.0025.
Values may be sent and summed in bfloat16 or wider, within the bound.
No kernel may reach another device: no remote copies, remote signals or barrier semaphores. Data moves between devices by JAX's collectives and lax.ppermute only.
A program may use at most 128 MiB of HBM per device.

v0:
```python
import jax
import jax.numpy as jnp
from jax import lax
from jax.sharding import PartitionSpec as P

STEPS = 4
CAP = 8
USERS_DEV = 32


def unit_rows(matrix):
    return (matrix * lax.rsqrt(jnp.sum(matrix * matrix, axis=1, keepdims=True) + 1e-06)).astype(
        jnp.bfloat16
    )


def project_in(inputs, gate_part, up_part):

    def add_rows(piece):
        return jnp.dot(inputs, piece, preferred_element_type=jnp.float32)

    gate = add_rows(lax.all_gather(gate_part, "user", axis=0, tiled=True))
    up_proj = add_rows(lax.all_gather(up_part, "user", axis=0, tiled=True))
    return (gate, up_proj)


def shards(
    states,
    norm_gain,
    gate_weight,
    up_weight,
    down_weight,
    proj_weight,
    private_rows,
    enc_weight,
    user_ids,
):
    tok_rows, width_model = states.shape
    groups = tok_rows // STEPS
    values = states.astype(jnp.float32)
    normed = (
        values * lax.rsqrt(jnp.mean(values * values, axis=1, keepdims=True) + 1e-05) * norm_gain
    ).astype(jnp.bfloat16)
    gate_part, up_part, down_part = (gate_weight, up_weight, down_weight)
    gate, up_proj = project_in(normed, gate_part, up_part)
    hidden = (jax.nn.silu(gate) * up_proj).astype(jnp.bfloat16)
    mixed = jnp.dot(
        hidden,
        lax.all_gather(down_part, "user", axis=1, tiled=True),
        preferred_element_type=jnp.float32,
    )
    pooled_mlp = jnp.sum(mixed.reshape(-1, STEPS, width_model), axis=1)
    pooled_mlp = lax.psum_scatter(pooled_mlp, "gen", scatter_dimension=1, tiled=True)
    slab_width = pooled_mlp.shape[1]
    own_cols = lax.dynamic_slice_in_dim(values, lax.axis_index("gen") * slab_width, slab_width, 1)
    pooled_in = jnp.sum(own_cols.reshape(groups, STEPS, slab_width), axis=1)
    pooled = ((pooled_in + pooled_mlp) / STEPS).astype(jnp.bfloat16)
    partial_emb = jnp.dot(pooled, proj_weight, preferred_element_type=jnp.float32)
    embedding = lax.psum(partial_emb, "gen")
    candidate = unit_rows(embedding)
    every_cand = lax.all_gather(candidate, "user", axis=0, tiled=True)
    encoded = unit_rows(jnp.dot(private_rows, enc_weight, preferred_element_type=jnp.float32))
    scores = lax.dot_general(
        encoded, every_cand, (((1,), (1,)), ((), ())), preferred_element_type=jnp.float32
    )
    kernel = jnp.exp(scores * 60.0)
    totals = lax.psum(jnp.sum(kernel, axis=1), "cand")
    member = (user_ids[:, None] == jnp.arange(USERS_DEV, dtype=jnp.int32)[None, :]).astype(
        jnp.float32
    )
    counts = jnp.sum(member, axis=0)
    limit = jnp.minimum(1.0, CAP / jnp.maximum(counts, 1.0))
    row_cap = jnp.dot(member, limit, precision=lax.Precision.HIGHEST)
    row_total = private_rows.shape[0] * lax.axis_size("gen") * lax.axis_size("user")
    cand_total = every_cand.shape[0] * lax.axis_size("cand")
    weight_rows = row_cap / totals * (cand_total / row_total)
    partial_votes = jnp.dot(weight_rows, kernel, precision=lax.Precision.HIGHEST)
    votes = lax.psum(partial_votes, ("gen", "user"))
    return votes.reshape(lax.axis_size("user"), 1, groups)


def solution(mesh):
    return jax.shard_map(
        shards,
        mesh=mesh,
        in_specs=(
            P(("user", "cand"), None),
            P(),
            P("user", "gen"),
            P("user", "gen"),
            P("gen", "user"),
            P("gen", None),
            P(("gen", "user"), None),
            P(),
            P(("gen", "user")),
        ),
        out_specs=P(None, "cand", None),
        check_vma=False,
    )
```

profile of v0, /device:TPU:0, one launch (start us, length us, event | category | flops | bytes accessed | tf_op | source)
XLA Modules:
  0.0 810.1 jit_solution(10870717847516051505)
XLA Ops:
  6.5 0.0 copy-start
  6.5 0.0 copy-start.1
  6.5 0.0 all-gather.5.cloned.1.call-start
  6.5 0.7 all-gather.5.cloned.1.call-update
  7.3 0.0 all-gather.7.cloned.1.call-start
  7.3 0.7 all-gather.7.cloned.1.call-update
  8.0 0.0 all-gather.9.cloned.1.call-start
  8.1 0.7 all-gather.9.cloned.1.call-update
  8.7 0.0 reduce-scatter.2.cloned.1.call-start
  8.8 3.1 multiply_reduce_fusion
  11.9 70.3 %all-gather.5.cloned.1.call-done = bf16[4096,896]{1,0:T(8,128)(2,1)} async-done(((bf16[256,896]{1,0:T(8,128)(2,1)}), bf16[4096,896]{1,0:T(8,128)(2,1)}) %all-gather.5.cloned.1.call-update) | async-done | bytes 7340048 | tf_op jit(solution)/shard_map/all_gather | solution.py:22
  82.2 0.0 copy-done.1
  82.2 10.1 %fusion.1 = f32[512,896]{1,0:T(8,128)} fusion(bf16[4096,896]{1,0:T(8,128)(2,1)} %all-gather.5.cloned.1.call-done, f32[4096]{0:T(1024)S(1)} %copy-done.1, f32[512]{0:T(512)S(1)} %add_rsqrt_fusion, bf16[512,4096]{1,0:T(8,128)(2,1)} %param.9), kind=kOutput, calls=%fused_computation.5 | convolution fusion | flops 3766484992 | bytes 13387776 | tf_op jit(solution)/shard_map/dot_general | solution.py:20
  92.3 63.2 %all-gather.7.cloned.1.call-done = bf16[4096,896]{1,0:T(8,128)(2,1)} async-done(((bf16[256,896]{1,0:T(8,128)(2,1)}), bf16[4096,896]{1,0:T(8,128)(2,1)}) %all-gather.7.cloned.1.call-update) | async-done | bytes 7340048 | tf_op jit(solution)/shard_map/all_gather | solution.py:23
  155.6 79.3 %all-gather.9.cloned.1.call-done = bf16[896,4096]{1,0:T(8,128)(2,1)} async-done(((bf16[896,256]{1,0:T(8,128)(2,1)}), bf16[896,4096]{1,0:T(8,128)(2,1)}) %all-gather.9.cloned.1.call-update) | async-done | bytes 7340048 | tf_op jit(solution)/shard_map/all_gather | solution.py:49
  234.8 17.4 %fusion.2 = f32[512,4096]{1,0:T(8,128)} fusion(bf16[896,4096]{1,0:T(8,128)(2,1)} %all-gather.9.cloned.1.call-done, f32[512,896]{1,0:T(8,128)} %fusion.1, bf16[4096,896]{1,0:T(8,128)(2,1)} %all-gather.7.cloned.1.call-done, f32[4096]{0:T(1024)S(1)} %copy-done.1, f32[512]{0:T(512)S(1)} %add_rsqrt_fusion, bf16[512,4096]{1,0:T(8,128)(2,1)} %param.9), kind=kOutput, calls=%fused_computation.9 | convolution fusion | flops 7527333888 | bytes 29116416 | tf_op jit(solution)/shard_map/dot_general | solution.py:47
  252.2 9.8 %reshape.32 = f32[128,4,4096]{2,1,0:T(4,128)} reshape(f32[512,4096]{1,0:T(8,128)} %fusion.2) | data formatting | bytes 16777216 | tf_op jit(solution)/shard_map/reshape | solution.py:52
  262.0 10.0 %reduce_sum.67 = f32[128,4096]{1,0:T(8,128)} reduce(f32[128,4,4096]{2,1,0:T(4,128)} %reshape.32, f32[]{:T(128)} %constant.15.clone.1), dimensions={1}, to_apply=%region_4.5 | reduce | flops 1572864 | bytes 10485764 | tf_op jit(solution)/shard_map/reduce_sum | solution.py:52
  272.0 0.0 reduce-scatter.2.cloned.1.call-update
  272.1 0.0 all-reduce.2.cloned.1.call-start
  272.1 6.5 convert_element_type.23
  278.6 1.3 constant_dynamic-slice_fusion
  279.9 0.0 copy-start.2
  279.9 1.3 reshape.31
  281.2 1.8 reduce_sum.65
  283.1 29.9 %reduce-scatter.2.cloned.1.call-done = f32[128,512]{1,0:T(8,128)} async-done(((f32[128,4096]{1,0:T(8,128)}), f32[128,512]{1,0:T(8,128)}) %reduce-scatter.2.cloned.1.call-update) | async-done | bytes 262160 | tf_op jit(solution)/shard_map/reduce_scatter | solution.py:53
  313.0 2.4 fusion.4
  315.4 0.0 all-reduce.2.cloned.1.call-update
  315.4 0.3 all-gather.11.cloned.1.call-start
  315.7 70.7 %all-reduce.2.cloned.1.call-done = f32[128,1024]{1,0:T(8,128)} async-done(((f32[128,1024]{1,0:T(8,128)}), f32[128,1024]{1,0:T(8,128)}) %all-reduce.2.cloned.1.call-update) | async-done | bytes 524304 | tf_op jit(solution)/shard_map/psum | solution.py:59
  386.3 1.2 multiply_reduce_fusion.2
  387.5 1.8 multiply_convert_fusion.8
  389.3 0.0 all-gather.11.cloned.1.call-update
  389.4 0.0 copy-done.2
  389.4 0.1 convert_reduce_fusion
  389.5 0.0 copy-done
  389.5 1.8 multiply_reduce_fusion.1
  391.3 0.1 fusion.6
  391.5 53.5 %all-gather.11.cloned.1.call-done = bf16[2048,1024]{1,0:T(8,128)(2,1)} async-done(((bf16[128,1024]{1,0:T(8,128)(2,1)}), bf16[2048,1024]{1,0:T(8,128)(2,1)}) %all-gather.11.cloned.1.call-update) | async-done | bytes 4194320 | tf_op jit(solution)/shard_map/all_gather | solution.py:61
  445.0 4.9 fusion.16
  449.8 8.8 %psum.22 = f32[256]{0:T(256)S(1)} all-reduce(f32[256]{0:T(256)S(1)} %get-tuple-element.7), channel_id=1, replica_groups=mesh['gen'=8,'user'=16,'cand'=2] {'cand'}, use_global_device_ids=true, to_apply=%region_9.10 | all-reduce | flops 256 | bytes 2048 | tf_op jit(solution)/shard_map/psum | solution.py:67
  458.6 2.7 convolution_bitcast_fusion
  461.3 341.9 %psum.23 = f32[16,1,128]{2,1,0:T(1,128)} all-reduce(f32[16,1,128]{2,1,0:T(1,128)S(1)} %convolution_bitcast_fusion), channel_id=1, replica_groups=mesh['gen'=8,'user'=16,'cand'=2] {'gen','user'}, use_global_device_ids=true, to_apply=%region_10.11 | all-reduce | flops 2048 | bytes 16384 | tf_op jit(solution)/shard_map/psum | solution.py:78
  (4 shorter events, 0.0 us)
Async XLA Ops:
  6.5 383.0 %copy-start = (bf16[1024,1024]{1,0:T(8,128)(2,1)S(1)}, bf16[1024,1024]{1,0:T(8,128)(2,1)}, u32[]{:S(2)}) copy-start(bf16[1024,1024]{1,0:T(8,128)(2,1)} %param.16) | copy-start | bytes 6291460
  6.5 75.7 %copy-start.1 = (f32[4096]{0:T(1024)S(1)}, f32[4096]{0:T(1024)}, u32[]{:S(2)}) copy-start(f32[4096]{0:T(1024)} %param.10) | copy-start | bytes 49156
  6.5 75.7 %all-gather.5.cloned.1.call-start = ((), (), s32[]{:S(2)}) async-start(), calls=%async_computation.1 | async-start | bytes 7798784 | tf_op jit(solution)/shard_map/all_gather | solution.py:22
  7.3 148.3 %all-gather.7.cloned.1.call-start = ((), (), s32[]{:S(2)}) async-start(), calls=%async_computation.2 | async-start | bytes 7798784 | tf_op jit(solution)/shard_map/all_gather | solution.py:23
  8.0 226.8 %all-gather.9.cloned.1.call-start = ((), (), s32[]{:S(2)}) async-start(), calls=%async_computation.3 | async-start | bytes 7798784 | tf_op jit(solution)/shard_map/all_gather | solution.py:49
  8.7 304.2 %reduce-scatter.2.cloned.1.call-start = ((), (), s32[]{:S(2)}) async-start(), calls=%async_computation.4 | async-start | bytes 2359296 | tf_op jit(solution)/shard_map/reduce_scatter | solution.py:53
  272.1 114.3 %all-reduce.2.cloned.1.call-start = ((), (), s32[]{:S(2)}) async-start(), calls=%async_computation.5 | async-start | bytes 1048576 | tf_op jit(solution)/shard_map/psum | solution.py:59
  279.9 109.5 %copy-start.2 = (s32[256]{0:T(256)S(1)}, s32[256]{0:T(256)}, u32[]{:S(2)}) copy-start(s32[256]{0:T(256)} %param.17) | copy-start | bytes 3076
  315.4 129.5 %all-gather.11.cloned.1.call-start = ((), (), s32[]{:S(2)}) async-start(), calls=%async_computation.6 | async-start | bytes 4456448 | tf_op jit(solution)/shard_map/all_gather | solution.py:61
Sparse Core Ops, SparseCore 0:
  9.8 72.3 all-gather.4
  84.7 70.8 all-gather.6
  158.0 76.7 all-gather.8
  272.2 40.7 reduce-scatter.1
  315.5 70.7 all-reduce.1
  389.5 55.4 all-gather.10
where the time goes:
time: 811 us; the launch traced here: 810 us
  waiting for transfers between devices  369 us (45%)
  blocking collectives  351 us (43%)
  matrix products  39.5 us (5%)
  other arithmetic  24.6 us (3%)
  between operations  13.5 us (2%)
  local copies, waits for them, and re-layouts  12.4 us (2%)
    psum x1, blocking collectives, shards(): votes = lax.psum(partial_votes, ('gen', 'user'))  342 us
    all_gather x1, waiting for transfers between devices, shards(): lax.all_gather(down_part, 'user', axis=1, tiled=True)  79.3 us
    psum x1, waiting for transfers between devices, shards(): embedding = lax.psum(partial_emb, 'gen')  70.7 us
    all_gather x1, waiting for transfers between devices, project_in(): gate = add_rows(lax.all_gather(gate_part, 'user', axis=0, tiled=True))  70.3 us
    all_gather x1, waiting for transfers between devices, project_in(): up_proj = add_rows(lax.all_gather(up_part, 'user', axis=0, tiled=True))  63.2 us
    all_gather x1, waiting for transfers between devices, shards(): every_cand = lax.all_gather(candidate, 'user', axis=0, tiled=True)  53.5 us
    reduce_scatter x1, waiting for transfers between devices, shards(): lax.psum_scatter(pooled_mlp, 'gen', scatter_dimension=1, tiled=True)  29.9 us
    dot_general x1, matrix products, shards(): jnp.dot(hidden, lax.all_gather(down_part, 'user', axis=1, tiled=True), pr...  17.4 us
  transfers between devices with their start and end apart: 6, of which 6 were waited for; matrix products, arithmetic and copies ran while one was open for 3% of the time, Pallas kernels for 0%

commit v1 on v0

--- a/solution.py
+++ b/solution.py
@@ -1,11 +1,32 @@
+import functools
 import jax
 import jax.numpy as jnp
 from jax import lax
 from jax.sharding import PartitionSpec as P
+from jax.lax import axis_index, axis_size, ppermute
 
 STEPS = 4
 CAP = 8
 USERS_DEV = 32
+
+
+def trace_the_works(frame_in, which_axis, d0):
+    lanes = axis_size(which_axis)
+    xs_all = tuple(((num, (num + 1) % lanes) for num in range(lanes)))
+    cards = tuple(((num, (num - 1) % lanes) for num in range(lanes)))
+    far_arr, arr_out = ([frame_in], [frame_in])
+    for _ in range(lanes // 2):
+        a_now = ppermute(far_arr[-1], which_axis, xs_all)
+        far_arr.append(a_now)
+    for _ in range((lanes - 1) // 2):
+        arr_out.append(ppermute(arr_out[-1], which_axis, cards))
+    v_next = jnp.concatenate([*far_arr[::-1], *arr_out[1:]], axis=d0)
+    return jnp.roll(
+        v_next, shift=(axis_index(which_axis) - lanes // 2) * frame_in.shape[d0], axis=d0
+    )
+
+
+modes_build = functools.partial(trace_the_works, which_axis="user", d0=1)
 
 
 def unit_rows(matrix):
@@ -44,11 +65,7 @@
     gate_part, up_part, down_part = (gate_weight, up_weight, down_weight)
     gate, up_proj = project_in(normed, gate_part, up_part)
     hidden = (jax.nn.silu(gate) * up_proj).astype(jnp.bfloat16)
-    mixed = jnp.dot(
-        hidden,
-        lax.all_gather(down_part, "user", axis=1, tiled=True),
-        preferred_element_type=jnp.float32,
-    )
+    mixed = jnp.dot(hidden, modes_build(down_part), preferred_element_type=jnp.float32)
     pooled_mlp = jnp.sum(mixed.reshape(-1, STEPS, width_model), axis=1)
     pooled_mlp = lax.psum_scatter(pooled_mlp, "gen", scatter_dimension=1, tiled=True)
     slab_width = pooled_mlp.shape[1]

time: 811 us -> 785 us (0.968)
  waiting for transfers between devices: 369 us -> 262 us
  local copies, waits for them, and re-layouts: 12.4 us -> 54.5 us
  starting transfers between devices: 0.42 us -> 38.4 us
    ppermute x0 -> x15, waiting for transfers between devices: none -> 112 us  [the longest x8 112 us: trace_the_works(): a_now = ppermute(far_arr[-1], which_axis, xs_all)]
    all_gather x1 -> x0, waiting for transfers between devices: 79.3 us -> none  [shards(): lax.all_gather(down_part, 'user', axis=1, tiled=True)]
    all_gather x1, waiting for transfers between devices: 70.3 us -> 0.01 us  [project_in(): gate = add_rows(lax.all_gather(gate_part, 'user', axis=0, tiled=True))]
    all_gather x1, waiting for transfers between devices: 63.2 us -> 0.01 us  [project_in(): up_proj = add_rows(lax.all_gather(up_part, 'user', axis=0, tiled=True))]
    unnamed x6 -> x63, local copies, waits for them, and re-layouts: 0.01 us -> 41.3 us
    ppermute x0 -> x15, starting transfers between devices: none -> 37.9 us  [the longest x7 37.8 us: trace_the_works(): arr_out.append(ppermute(arr_out[-1], which_axis, cards))]
  transfers between devices with their start and end apart: 6 -> 20, of which waited for: 6 -> 11; matrix products, arithmetic and copies ran while one was open for 3% -> 9% of each run, Pallas kernels for 0% -> 0%
where the time goes in v1:
time: 785 us; the launch traced here: 783 us
  blocking collectives  351 us (45%)
  waiting for transfers between devices  262 us (33%)
  local copies, waits for them, and re-layouts  54.5 us (7%)
  matrix products  39.5 us (5%)
  starting transfers between devices  38.4 us (5%)
  other arithmetic  24.6 us (3%)
  between operations  13.3 us (2%)
    psum x1, blocking collectives, shards(): votes = lax.psum(partial_votes, ('gen', 'user'))  342 us
    ppermute x8, waiting for transfers between devices, trace_the_works(): a_now = ppermute(far_arr[-1], which_axis, xs_all)  112 us
    psum x1, waiting for transfers between devices, shards(): embedding = lax.psum(partial_emb, 'gen')  70.7 us
    all_gather x1, waiting for transfers between devices, shards(): every_cand = lax.all_gather(candidate, 'user', axis=0, tiled=True)  53.5 us
    unnamed x63, local copies, waits for them, and re-layouts  41.3 us
    ppermute x7, starting transfers between devices, trace_the_works(): arr_out.append(ppermute(arr_out[-1], which_axis, cards))  37.8 us
    reduce_scatter x1, waiting for transfers between devices, shards(): lax.psum_scatter(pooled_mlp, 'gen', scatter_dimension=1, tiled=True)  24.8 us
    dot_general x1, matrix products, shards(): jnp.dot(hidden, modes_build(down_part), preferred_element_type=jnp.float32)  17.4 us
  transfers between devices with their start and end apart: 20, of which 11 were waited for; matrix products, arithmetic and copies ran while one was open for 9% of the time, Pallas kernels for 0%

profile of v1, /device:TPU:0, one launch (start us, length us, event | category | flops | bytes accessed | tf_op | source)
XLA Modules:
  0.0 783.3 jit_solution(1010670928891532978)
XLA Ops:
  8.1 14.2 %collective-permute-done = bf16[896,256]{1,0:T(8,128)(2,1)S(1)} collective-permute-done((bf16[896,256]{1,0:T(8,128)(2,1)}, bf16[896,256]{1,0:T(8,128)(2,1)S(1)}, u32[]{:S(2)}, u32[]{:S(2)}) %collective-permute-start) | collective-permute-done | bytes 458784 | tf_op jit(solution)/shard_map/ppermute | solution.py:19
  22.4 5.3 collective-permute-start.8
  27.7 16.3 %collective-permute-done.1 = bf16[896,256]{1,0:T(8,128)(2,1)S(1)} collective-permute-done((bf16[896,256]{1,0:T(8,128)(2,1)S(1)}, bf16[896,256]{1,0:T(8,128)(2,1)S(1)}, u32[]{:S(2)}, u32[]{:S(2)}) %collective-permute-start.1) | collective-permute-done | bytes 458784 | tf_op jit(solution)/shard_map/ppermute | solution.py:19
  44.0 5.3 collective-permute-start.9
  49.4 8.7 %collective-permute-done.2 = bf16[896,256]{1,0:T(8,128)(2,1)S(1)} collective-permute-done((bf16[896,256]{1,0:T(8,128)(2,1)S(1)}, bf16[896,256]{1,0:T(8,128)(2,1)S(1)}, u32[]{:S(2)}, u32[]{:S(2)}) %collective-permute-start.2) | collective-permute-done | bytes 458784 | tf_op jit(solution)/shard_map/ppermute | solution.py:19
  58.1 5.4 collective-permute-start.10
  63.5 20.8 %collective-permute-done.3 = bf16[896,256]{1,0:T(8,128)(2,1)S(1)} collective-permute-done((bf16[896,256]{1,0:T(8,128)(2,1)S(1)}, bf16[896,256]{1,0:T(8,128)(2,1)S(1)}, u32[]{:S(2)}, u32[]{:S(2)}) %collective-permute-start.3) | collective-permute-done | bytes 458784 | tf_op jit(solution)/shard_map/ppermute | solution.py:19
  84.3 5.4 collective-permute-start.11
  89.7 21.0 %collective-permute-done.4 = bf16[896,256]{1,0:T(8,128)(2,1)S(1)} collective-permute-done((bf16[896,256]{1,0:T(8,128)(2,1)S(1)}, bf16[896,256]{1,0:T(8,128)(2,1)S(1)}, u32[]{:S(2)}, u32[]{:S(2)}) %collective-permute-start.4) | collective-permute-done | bytes 458784 | tf_op jit(solution)/shard_map/ppermute | solution.py:19
  110.7 5.3 collective-permute-start.12
  116.0 10.8 %collective-permute-done.5 = bf16[896,256]{1,0:T(8,128)(2,1)} collective-permute-done((bf16[896,256]{1,0:T(8,128)(2,1)S(1)}, bf16[896,256]{1,0:T(8,128)(2,1)}, u32[]{:S(2)}, u32[]{:S(2)}) %collective-permute-start.5) | collective-permute-done | bytes 458784 | tf_op jit(solution)/shard_map/ppermute | solution.py:19
  126.9 5.4 collective-permute-start.13
  132.3 16.8 %collective-permute-done.6 = bf16[896,256]{1,0:T(8,128)(2,1)} collective-permute-done((bf16[896,256]{1,0:T(8,128)(2,1)}, bf16[896,256]{1,0:T(8,128)(2,1)}, u32[]{:S(2)}, u32[]{:S(2)}) %collective-permute-start.6) | collective-permute-done | bytes 458784 | tf_op jit(solution)/shard_map/ppermute | solution.py:19
  149.1 3.1 multiply_reduce_fusion
  152.2 5.6 collective-permute-start.14
  157.8 3.3 collective-permute-done.7
  161.1 0.9 constant_dynamic-update-slice_fusion.31
  162.0 1.9 constant_dynamic-update-slice_fusion.30
  163.9 1.9 constant_dynamic-update-slice_fusion.29
  165.7 1.9 constant_dynamic-update-slice_fusion.28
  167.6 1.9 constant_dynamic-update-slice_fusion.27
  169.6 1.9 constant_dynamic-update-slice_fusion.26
  171.5 1.9 constant_dynamic-update-slice_fusion.25
  173.3 0.9 constant_dynamic-update-slice_fusion.24
  174.2 1.9 constant_dynamic-update-slice_fusion.23
  176.9 1.9 constant_dynamic-update-slice_fusion.21
  178.7 1.9 constant_dynamic-update-slice_fusion.20
  180.6 1.8 constant_dynamic-update-slice_fusion.19
  182.4 1.9 constant_dynamic-update-slice_fusion.18
  184.3 0.8 constant_dynamic-update-slice_fusion.17
  185.1 0.8 constant_dynamic-update-slice_fusion.16
  186.0 0.8 constant_dynamic-update-slice_fusion.15
  186.8 1.8 constant_dynamic-update-slice_fusion.14
  188.6 1.8 constant_dynamic-update-slice_fusion.13
  190.5 0.8 constant_dynamic-update-slice_fusion.12
  191.3 0.8 constant_dynamic-update-slice_fusion.11
  192.1 0.8 constant_dynamic-update-slice_fusion.10
  192.9 0.8 constant_dynamic-update-slice_fusion.9
  194.6 0.8 constant_dynamic-update-slice_fusion.7
  195.4 0.8 constant_dynamic-update-slice_fusion.6
  196.2 0.8 constant_dynamic-update-slice_fusion.5
  197.8 1.8 constant_dynamic-update-slice_fusion.3
  199.7 1.8 constant_dynamic-update-slice_fusion.2
  201.5 0.8 constant_dynamic-update-slice_fusion.1
  202.3 0.8 constant_dynamic-update-slice_fusion
  203.2 10.1 %fusion.3 = f32[512,896]{1,0:T(8,128)} fusion(bf16[4096,896]{1,0:T(8,128)(2,1)} %all-gather.4.cloned.1.call-done, f32[4096]{0:T(1024)S(1)} %copy-done.14, f32[512]{0:T(512)S(1)} %add_rsqrt_fusion, bf16[512,4096]{1,0:T(8,128)(2,1)} %param.9), kind=kOutput, calls=%fused_computation.7 | convolution fusion | flops 3766484992 | bytes 13387776 | tf_op jit(solution)/shard_map/dot_general | solution.py:41
  213.3 17.4 %fusion = f32[512,4096]{1,0:T(8,128)} fusion(bf16[896,8192]{1,0:T(8,128)(2,1)} %constant_dynamic-update-slice_fusion, s32[]{:T(128)S(6)} %select_n.18, f32[512,896]{1,0:T(8,128)} %fusion.3, bf16[4096,896]{1,0:T(8,128)(2,1)} %all-gather.6.cloned.1.call-done, f32[4096]{0:T(1024)S(1)} %copy-done.14, f32[512]{0:T(512)S(1)} %add_rsqrt_fusion, ...), kind=kOutput, calls=%fused_computation.2 | convolution fusion | flops 7527333888 | bytes 29116420 | tf_op jit(solution)/shard_map/dot_general | solution.py:68
  230.7 9.8 %reshape.32 = f32[128,4,4096]{2,1,0:T(4,128)} reshape(f32[512,4096]{1,0:T(8,128)} %fusion) | data formatting | bytes 16777216 | tf_op jit(solution)/shard_map/reshape | solution.py:69
  240.5 10.1 %reduce_sum.67 = f32[128,4096]{1,0:T(8,128)} reduce(f32[128,4,4096]{2,1,0:T(4,128)} %reshape.32, f32[]{:T(128)} %constant.23.clone.1), dimensions={1}, to_apply=%region_4.5 | reduce | flops 1572864 | bytes 10485764 | tf_op jit(solution)/shard_map/reduce_sum | solution.py:69
  250.7 6.5 convert_element_type.23
  257.2 1.3 constant_dynamic-slice_fusion
  258.5 1.3 reshape.31
  259.8 1.8 reduce_sum.65
  261.6 24.8 %reduce-scatter.2.cloned.1.call-done = f32[128,512]{1,0:T(8,128)} async-done(((f32[128,4096]{1,0:T(8,128)}), f32[128,512]{1,0:T(8,128)}) %reduce-scatter.2.cloned.1.call-update) | async-done | bytes 262160 | tf_op jit(solution)/shard_map/reduce_scatter | solution.py:70
  286.4 2.4 fusion.5
  289.2 70.7 %all-reduce.2.cloned.1.call-done = f32[128,1024]{1,0:T(8,128)} async-done(((f32[128,1024]{1,0:T(8,128)}), f32[128,1024]{1,0:T(8,128)}) %all-reduce.2.cloned.1.call-update) | async-done | bytes 524304 | tf_op jit(solution)/shard_map/psum | solution.py:76
  359.8 1.2 multiply_reduce_fusion.2
  361.0 1.8 multiply_convert_fusion.8
  363.0 1.8 multiply_reduce_fusion.1
  365.0 53.5 %all-gather.8.cloned.1.call-done = bf16[2048,1024]{1,0:T(8,128)(2,1)} async-done(((bf16[128,1024]{1,0:T(8,128)(2,1)}), bf16[2048,1024]{1,0:T(8,128)(2,1)}) %all-gather.8.cloned.1.call-update) | async-done | bytes 4194320 | tf_op jit(solution)/shard_map/all_gather | solution.py:78
  418.5 4.9 fusion.18
  423.3 8.8 %psum.22 = f32[256]{0:T(256)S(1)} all-reduce(f32[256]{0:T(256)S(1)} %get-tuple-element.7), channel_id=1, replica_groups=mesh['gen'=8,'user'=16,'cand'=2] {'cand'}, use_global_device_ids=true, to_apply=%region_9.10 | all-reduce | flops 256 | bytes 2048 | tf_op jit(solution)/shard_map/psum | solution.py:84
  432.2 2.7 convolution_bitcast_fusion
  434.8 341.9 %psum.23 = f32[16,1,128]{2,1,0:T(1,128)} all-reduce(f32[16,1,128]{2,1,0:T(1,128)S(1)} %convolution_bitcast_fusion), channel_id=1, replica_groups=mesh['gen'=8,'user'=16,'cand'=2] {'gen','user'}, use_global_device_ids=true, to_apply=%region_10.11 | all-reduce | flops 2048 | bytes 16384 | tf_op jit(solution)/shard_map/psum | solution.py:95
  (68 shorter events, 4.8 us)
Async XLA Ops:
  6.5 356.5 %copy-start = (bf16[1024,1024]{1,0:T(8,128)(2,1)S(1)}, bf16[1024,1024]{1,0:T(8,128)(2,1)}, u32[]{:S(2)}) copy-start(bf16[1024,1024]{1,0:T(8,128)(2,1)} %param.16) | copy-start | bytes 6291460
  6.5 188.0 %copy-start.1 = (bf16[896,256]{1,0:T(8,128)(2,1)S(1)}, bf16[896,256]{1,0:T(8,128)(2,1)}, u32[]{:S(2)}) copy-start(bf16[896,256]{1,0:T(8,128)(2,1)} %param.13) | copy-start | bytes 1376260
  6.5 196.7 %all-gather.4.cloned.1.call-start = ((), (), s32[]{:S(2)}) async-start(), calls=%async_computation.1 | async-start | bytes 7798784 | tf_op jit(solution)/shard_map/all_gather | solution.py:43
  7.3 206.0 %all-gather.6.cloned.1.call-start = ((), (), s32[]{:S(2)}) async-start(), calls=%async_computation.2 | async-start | bytes 7798784 | tf_op jit(solution)/shard_map/all_gather | solution.py:44
  8.0 278.4 %reduce-scatter.2.cloned.1.call-start = ((), (), s32[]{:S(2)}) async-start(), calls=%async_computation.3 | async-start | bytes 2359296 | tf_op jit(solution)/shard_map/reduce_scatter | solution.py:70
  8.1 14.3 %collective-permute-start = (bf16[896,256]{1,0:T(8,128)(2,1)}, bf16[896,256]{1,0:T(8,128)(2,1)S(1)}, u32[]{:S(2)}, u32[]{:S(2)}) collective-permute-start(bf16[896,256]{1,0:T(8,128)(2,1)} %param.13), channel_id=1, source_target_pairs={{0,2},{2,4},{4,6},{6,8},{8,10},{10,12},{12,14},{14,16},{16,18},{18... | collective-permute-start | bytes 1376264 | tf_op jit(solution)/shard_map/ppermute | solution.py:19
  22.4 21.7 %collective-permute-start.1 = (bf16[896,256]{1,0:T(8,128)(2,1)S(1)}, bf16[896,256]{1,0:T(8,128)(2,1)S(1)}, u32[]{:S(2)}, u32[]{:S(2)}) collective-permute-start(bf16[896,256]{1,0:T(8,128)(2,1)S(1)} %collective-permute-done), channel_id=1, source_target_pairs={{0,2},{2,4},{4,6},{6,8},{8,10},{10,12},{12,14},{14,16},{16,18},{18... | collective-permute-start | bytes 1376264 | tf_op jit(solution)/shard_map/ppermute | solution.py:19
  22.4 21.7 %collective-permute-start.8 = (bf16[896,256]{1,0:T(8,128)(2,1)}, bf16[896,256]{1,0:T(8,128)(2,1)S(1)}, u32[]{:S(2)}, u32[]{:S(2)}) collective-permute-start(bf16[896,256]{1,0:T(8,128)(2,1)} %param.13), channel_id=1, source_target_pairs={{0,30},{2,0},{4,2},{6,4},{8,6},{10,8},{12,10},{14,12},{16,14},{18,... | collective-permute-start | bytes 1376264 | tf_op jit(solution)/shard_map/ppermute | solution.py:22
  44.0 14.1 %copy-start.2 = (bf16[896,256]{1,0:T(8,128)(2,1)}, bf16[896,256]{1,0:T(8,128)(2,1)S(1)}, u32[]{:S(2)}) copy-start(bf16[896,256]{1,0:T(8,128)(2,1)S(1)} %collective-permute-done.1) | copy-start | bytes 1376260
  44.0 14.1 %collective-permute-start.2 = (bf16[896,256]{1,0:T(8,128)(2,1)S(1)}, bf16[896,256]{1,0:T(8,128)(2,1)S(1)}, u32[]{:S(2)}, u32[]{:S(2)}) collective-permute-start(bf16[896,256]{1,0:T(8,128)(2,1)S(1)} %collective-permute-done.1), channel_id=1, source_target_pairs={{0,2},{2,4},{4,6},{6,8},{8,10},{10,12},{12,14},{14,16},{16,18},{18... | collective-permute-start | bytes 1376264 | tf_op jit(solution)/shard_map/ppermute | solution.py:19
  44.0 14.1 %collective-permute-start.9 = (bf16[896,256]{1,0:T(8,128)(2,1)S(1)}, bf16[896,256]{1,0:T(8,128)(2,1)S(1)}, u32[]{:S(2)}, u32[]{:S(2)}) collective-permute-start(bf16[896,256]{1,0:T(8,128)(2,1)S(1)} %collective-permute-done.8), channel_id=1, source_target_pairs={{0,30},{2,0},{4,2},{6,4},{8,6},{10,8},{12,10},{14,12},{16,14},{18,... | collective-permute-start | bytes 1376264 | tf_op jit(solution)/shard_map/ppermute | solution.py:22
  58.1 26.2 %copy-start.6 = (bf16[896,256]{1,0:T(8,128)(2,1)}, bf16[896,256]{1,0:T(8,128)(2,1)S(1)}, u32[]{:S(2)}) copy-start(bf16[896,256]{1,0:T(8,128)(2,1)S(1)} %collective-permute-done.2) | copy-start | bytes 1376260
  58.1 26.2 %collective-permute-start.3 = (bf16[896,256]{1,0:T(8,128)(2,1)S(1)}, bf16[896,256]{1,0:T(8,128)(2,1)S(1)}, u32[]{:S(2)}, u32[]{:S(2)}) collective-permute-start(bf16[896,256]{1,0:T(8,128)(2,1)S(1)} %collective-permute-done.2), channel_id=1, source_target_pairs={{0,2},{2,4},{4,6},{6,8},{8,10},{10,12},{12,14},{14,16},{16,18},{18... | collective-permute-start | bytes 1376264 | tf_op jit(solution)/shard_map/ppermute | solution.py:19
  58.1 5.4 copy-start.4
  58.1 26.2 %collective-permute-start.10 = (bf16[896,256]{1,0:T(8,128)(2,1)S(1)}, bf16[896,256]{1,0:T(8,128)(2,1)S(1)}, u32[]{:S(2)}, u32[]{:S(2)}) collective-permute-start(bf16[896,256]{1,0:T(8,128)(2,1)S(1)} %collective-permute-done.9), channel_id=1, source_target_pairs={{0,30},{2,0},{4,2},{6,4},{8,6},{10,8},{12,10},{14,12},{16,14},{18,... | collective-permute-start | bytes 1376264 | tf_op jit(solution)/shard_map/ppermute | solution.py:22
  84.3 26.4 %copy-start.10 = (bf16[896,256]{1,0:T(8,128)(2,1)}, bf16[896,256]{1,0:T(8,128)(2,1)S(1)}, u32[]{:S(2)}) copy-start(bf16[896,256]{1,0:T(8,128)(2,1)S(1)} %collective-permute-done.3) | copy-start | bytes 1376260
  84.3 26.4 %collective-permute-start.4 = (bf16[896,256]{1,0:T(8,128)(2,1)S(1)}, bf16[896,256]{1,0:T(8,128)(2,1)S(1)}, u32[]{:S(2)}, u32[]{:S(2)}) collective-permute-start(bf16[896,256]{1,0:T(8,128)(2,1)S(1)} %collective-permute-done.3), channel_id=1, source_target_pairs={{0,2},{2,4},{4,6},{6,8},{8,10},{10,12},{12,14},{14,16},{16,18},{18... | collective-permute-start | bytes 1376264 | tf_op jit(solution)/shard_map/ppermute | solution.py:19
  84.3 5.4 copy-start.8
  84.3 26.4 %collective-permute-start.11 = (bf16[896,256]{1,0:T(8,128)(2,1)S(1)}, bf16[896,256]{1,0:T(8,128)(2,1)}, u32[]{:S(2)}, u32[]{:S(2)}) collective-permute-start(bf16[896,256]{1,0:T(8,128)(2,1)S(1)} %collective-permute-done.10), channel_id=1, source_target_pairs={{0,30},{2,0},{4,2},{6,4},{8,6},{10,8},{12,10},{14,12},{16,14},{18,... | collective-permute-start | bytes 1376264 | tf_op jit(solution)/shard_map/ppermute | solution.py:22
  110.7 5.4 copy-start.12
  110.7 16.2 %collective-permute-start.5 = (bf16[896,256]{1,0:T(8,128)(2,1)S(1)}, bf16[896,256]{1,0:T(8,128)(2,1)}, u32[]{:S(2)}, u32[]{:S(2)}) collective-permute-start(bf16[896,256]{1,0:T(8,128)(2,1)S(1)} %collective-permute-done.4), channel_id=1, source_target_pairs={{0,2},{2,4},{4,6},{6,8},{8,10},{10,12},{12,14},{14,16},{16,18},{18... | collective-permute-start | bytes 1376264 | tf_op jit(solution)/shard_map/ppermute | solution.py:19
  110.7 16.2 %collective-permute-start.12 = (bf16[896,256]{1,0:T(8,128)(2,1)}, bf16[896,256]{1,0:T(8,128)(2,1)}, u32[]{:S(2)}, u32[]{:S(2)}) collective-permute-start(bf16[896,256]{1,0:T(8,128)(2,1)} %collective-permute-done.11), channel_id=1, source_target_pairs={{0,30},{2,0},{4,2},{6,4},{8,6},{10,8},{12,10},{14,12},{16,14},{18,... | collective-permute-start | bytes 1376264 | tf_op jit(solution)/shard_map/ppermute | solution.py:22
  126.9 22.2 %collective-permute-start.6 = (bf16[896,256]{1,0:T(8,128)(2,1)}, bf16[896,256]{1,0:T(8,128)(2,1)}, u32[]{:S(2)}, u32[]{:S(2)}) collective-permute-start(bf16[896,256]{1,0:T(8,128)(2,1)} %collective-permute-done.5), channel_id=1, source_target_pairs={{0,2},{2,4},{4,6},{6,8},{8,10},{10,12},{12,14},{14,16},{16,18},{18... | collective-permute-start | bytes 1376264 | tf_op jit(solution)/shard_map/ppermute | solution.py:19
  126.9 63.6 %copy-start.13 = (bf16[896,256]{1,0:T(8,128)(2,1)S(1)}, bf16[896,256]{1,0:T(8,128)(2,1)}, u32[]{:S(2)}) copy-start(bf16[896,256]{1,0:T(8,128)(2,1)} %copy-done.12) | copy-start | bytes 1376260
  126.9 64.4 %copy-start.11 = (bf16[896,256]{1,0:T(8,128)(2,1)S(1)}, bf16[896,256]{1,0:T(8,128)(2,1)}, u32[]{:S(2)}) copy-start(bf16[896,256]{1,0:T(8,128)(2,1)} %copy-done.10) | copy-start | bytes 1376260
  126.9 65.3 %copy-start.7 = (bf16[896,256]{1,0:T(8,128)(2,1)S(1)}, bf16[896,256]{1,0:T(8,128)(2,1)}, u32[]{:S(2)}) copy-start(bf16[896,256]{1,0:T(8,128)(2,1)} %copy-done.6) | copy-start | bytes 1376260
  126.9 66.1 %copy-start.3 = (bf16[896,256]{1,0:T(8,128)(2,1)S(1)}, bf16[896,256]{1,0:T(8,128)(2,1)}, u32[]{:S(2)}) copy-start(bf16[896,256]{1,0:T(8,128)(2,1)} %copy-done.2) | copy-start | bytes 1376260
  126.9 69.3 %copy-start.5 = (bf16[896,256]{1,0:T(8,128)(2,1)S(1)}, bf16[896,256]{1,0:T(8,128)(2,1)}, u32[]{:S(2)}) copy-start(bf16[896,256]{1,0:T(8,128)(2,1)} %copy-done.4) | copy-start | bytes 1376260
  126.9 70.2 %copy-start.9 = (bf16[896,256]{1,0:T(8,128)(2,1)S(1)}, bf16[896,256]{1,0:T(8,128)(2,1)}, u32[]{:S(2)}) copy-start(bf16[896,256]{1,0:T(8,128)(2,1)} %copy-done.8) | copy-start | bytes 1376260
  126.9 25.3 %collective-permute-start.13 = (bf16[896,256]{1,0:T(8,128)(2,1)}, bf16[896,256]{1,0:T(8,128)(2,1)S(1)}, u32[]{:S(2)}, u32[]{:S(2)}) collective-permute-start(bf16[896,256]{1,0:T(8,128)(2,1)} %collective-permute-done.12), channel_id=1, source_target_pairs={{0,30},{2,0},{4,2},{6,4},{8,6},{10,8},{12,10},{14,12},{16,14},{18,... | collective-permute-start | bytes 1376264 | tf_op jit(solution)/shard_map/ppermute | solution.py:22
  149.1 12.0 %collective-permute-start.7 = (bf16[896,256]{1,0:T(8,128)(2,1)}, bf16[896,256]{1,0:T(8,128)(2,1)S(1)}, u32[]{:S(2)}, u32[]{:S(2)}) collective-permute-start(bf16[896,256]{1,0:T(8,128)(2,1)} %collective-permute-done.6), channel_id=1, source_target_pairs={{0,2},{2,4},{4,6},{6,8},{8,10},{10,12},{12,14},{14,16},{16,18},{18... | collective-permute-start | bytes 1376264 | tf_op jit(solution)/shard_map/ppermute | solution.py:19
  152.2 51.0 %copy-start.14 = (f32[4096]{0:T(1024)S(1)}, f32[4096]{0:T(1024)}, u32[]{:S(2)}) copy-start(f32[4096]{0:T(1024)} %param.10) | copy-start | bytes 49156
  152.2 32.9 %collective-permute-start.14 = (bf16[896,256]{1,0:T(8,128)(2,1)S(1)}, bf16[896,256]{1,0:T(8,128)(2,1)S(1)}, u32[]{:S(2)}, u32[]{:S(2)}) collective-permute-start(bf16[896,256]{1,0:T(8,128)(2,1)S(1)} %collective-permute-done.13), channel_id=1, source_target_pairs={{0,30},{2,0},{4,2},{6,4},{8,6},{10,8},{12,10},{14,12},{16,14},{18,... | collective-permute-start | bytes 1376264 | tf_op jit(solution)/shard_map/ppermute | solution.py:22
  250.6 112.3 %copy-start.15 = (s32[256]{0:T(256)S(1)}, s32[256]{0:T(256)}, u32[]{:S(2)}) copy-start(s32[256]{0:T(256)} %param.17) | copy-start | bytes 3076
  250.6 109.2 %all-reduce.2.cloned.1.call-start = ((), (), s32[]{:S(2)}) async-start(), calls=%async_computation.4 | async-start | bytes 1048576 | tf_op jit(solution)/shard_map/psum | solution.py:76
  288.8 129.6 %all-gather.8.cloned.1.call-start = ((), (), s32[]{:S(2)}) async-start(), calls=%async_computation.5 | async-start | bytes 4456448 | tf_op jit(solution)/shard_map/all_gather | solution.py:78
Sparse Core Ops, SparseCore 0:
  9.8 99.3 all-gather.3
  111.7 81.6 all-gather.5
  250.8 35.5 reduce-scatter.1
  289.0 70.8 all-reduce.1
  363.0 55.4 all-gather.7
